TPU v7x, 32 devices: a whole 2x2x4 slice. The times are simulated.
32 devices in a mesh: dp: 16 (over z, y, core), tensor: 2 (over x).
Axes of the slice: x: 2, y: 2, z: 4, core: 2. Of those that a mesh axis runs over, the one named last changes fastest.
Arguments:
- clip_feats: bfloat16 [2048, 1280], P('dp', 'tensor'), may hold values from -3 to 3
- proj_weight: bfloat16 [1280, 512], P('tensor'), may hold values from -1 to 1
- caption_emb: bfloat16 [2048, 512], P(('dp', 'tensor')), may hold values from -1.25 to 1.25
- logit_scale: float32 [1], replicated, may hold values from 20 to 400
- pair_perm: int32 [2048], replicated, may hold values from 0 to 2047, as said below
Outputs:
- clip_grad: float32 [2048, 1280], P('dp', 'tensor')
- caption_grad: float32 [2048, 512], P(('dp', 'tensor'))
- row_loss: float32 [2048], P('dp')
Inputs may be any that keep to these rules, and one draw needn't show every extreme that they name: pair_perm is a permutation of the 2048 caption indices.
All inputs are finite; a program needn't handle non-finite values.
Results may differ from a plain program's by a relative error of at most 0.012.
The roundings to bfloat16 on the way count: a program that leaves them out, or rounds other values in their place, can miss the bound.
Values may be sent and summed in bfloat16 or wider, within the bound.
A program may use at most 64 MiB of HBM per device.

v0:
```python
import jax
import jax.numpy as jnp
from jax import lax
from jax.sharding import PartitionSpec as P

norm_eps = 1e-06


def unit_rows(values):
    squares = jnp.sum(values * values, axis=1, keepdims=True)
    inverse = lax.rsqrt(squares + norm_eps)
    return (values * inverse, inverse)


def score_slab(videos, slab_rows, offset, target, logit):
    scores = logit * lax.dot_general(
        videos, slab_rows, (((1,), (1,)), ((), ())), preferred_element_type=jnp.float32
    )
    column = offset + jnp.arange(slab_rows.shape[0], dtype=jnp.int32)
    onehot = (column[None, :] == target[:, None]).astype(jnp.float32)
    return (scores, onehot)


def fold_stats(carry, slab_rows, offset, videos, target, logit):
    run_max, run_sum, run_pos = carry
    scores, onehot = score_slab(videos, slab_rows, offset, target, logit)
    new_max = jnp.maximum(run_max, jnp.max(scores, axis=1))
    run_sum = jnp.sum(jnp.exp(scores - new_max[:, None]), axis=1)
    run_pos = jnp.sum(scores * onehot, axis=1)
    return (new_max, run_sum, run_pos)


def slab_weights(slab_rows, offset, videos, target, logit, row_max, row_sum):
    scores, onehot = score_slab(videos, slab_rows, offset, target, logit)
    weights = (jnp.exp(scores - row_max[:, None]) / row_sum[:, None] - onehot).astype(jnp.bfloat16)
    vid_part = logit * jnp.dot(weights, slab_rows, preferred_element_type=jnp.float32)
    return (weights, vid_part)


def body(clip_feats, proj_weight, caption_emb, logit_scale, pair_perm):
    logit = logit_scale[0]
    partial_value = jnp.dot(clip_feats, proj_weight, preferred_element_type=jnp.float32)
    raw_proj = lax.psum(partial_value, "tensor")
    unit_vid, vid_inv = unit_rows(raw_proj)
    videos = unit_vid.astype(jnp.bfloat16)
    cap_unit, cap_inv = unit_rows(caption_emb.astype(jnp.float32))
    captions = cap_unit.astype(jnp.bfloat16)
    row_count = videos.shape[0]
    cap_count = captions.shape[0]
    groups = lax.axis_size("tensor")
    tensor_pos = lax.axis_index("tensor")
    wanted = lax.dynamic_slice_in_dim(pair_perm, lax.axis_index("dp") * row_count, row_count, 0)
    owner_block = wanted // cap_count
    local_col = owner_block // groups * cap_count + wanted % cap_count
    target = jnp.where(owner_block % groups == tensor_pos, local_col, -1)
    start_stats = (
        jnp.full((row_count,), -1e30, jnp.float32),
        jnp.zeros((row_count,), jnp.float32),
        jnp.zeros((row_count,), jnp.float32),
    )
    gathered = lax.all_gather(captions, "dp", axis=0, tiled=True)
    stats = fold_stats(start_stats, gathered, 0, videos, target, logit)
    row_max = lax.pmax(stats[0], "tensor")
    row_sum, row_pos = lax.psum((stats[1] * jnp.exp(stats[0] - row_max), stats[2]), "tensor")
    losses = row_max + jnp.log(row_sum) - row_pos
    weights_all, vid_part = slab_weights(gathered, 0, videos, target, logit, row_max, row_sum)
    vid_grad = lax.psum(vid_part, "tensor")
    cap_part = logit * lax.dot_general(
        weights_all, videos, (((0,), (0,)), ((), ())), preferred_element_type=jnp.float32
    )
    cap_grad = lax.psum_scatter(cap_part, "dp", scatter_dimension=0, tiled=True)
    vid_dot = jnp.sum(unit_vid * vid_grad, axis=1, keepdims=True)
    raw_grad = ((vid_grad - unit_vid * vid_dot) * vid_inv).astype(jnp.bfloat16)
    clip_grad = lax.dot_general(
        raw_grad, proj_weight, (((1,), (1,)), ((), ())), preferred_element_type=jnp.float32
    )
    cap_dot = jnp.sum(cap_unit * cap_grad, axis=1, keepdims=True)
    caption_grad = (cap_grad - cap_unit * cap_dot) * cap_inv
    return (clip_grad, caption_grad, losses)


def solution(mesh):
    return jax.shard_map(
        body,
        mesh=mesh,
        in_specs=(P("dp", "tensor"), P("tensor", None), P(("dp", "tensor"), None), P(), P()),
        out_specs=(P("dp", "tensor"), P(("dp", "tensor"), None), P("dp")),
        check_vma=False,
    )
```

profile of v0, /device:TPU:0, one launch (start us, length us, event | category | flops | bytes accessed | tf_op | source)
XLA Modules:
  0.0 143.4 jit_solution(11747821214149107070)
XLA Ops:
  8.0 0.0 copy-start
  8.0 0.0 all-reduce.4.cloned.1.call-start
  8.1 1.0 copy-done
  9.1 1.9 %fusion.12 = f32[128,512]{1,0:T(8,128)} fusion(bf16[128,640]{1,0:T(8,128)(2,1)} %param.5, bf16[640,512]{1,0:T(8,128)(2,1)S(1)} %copy-done), kind=kOutput, calls=%fused_computation.41 | convolution fusion | flops 83886080 | bytes 1081344 | tf_op jit(solution)/shard_map/dot_general | solution.py:42
  11.0 0.0 all-reduce.4.cloned.1.call-update
  11.0 0.0 all-gather.2.cloned.1.call-start
  11.1 1.0 fusion.6
  12.0 1.6 %fusion.2 = bf16[64,512]{1,0:T(8,128)(2,1)} fusion(bf16[64,512]{1,0:T(8,128)(2,1)} %param.7, f32[64]{0:T(128)S(1)} %add_rsqrt_fusion), kind=kLoop, calls=%fused_computation.15 | loop fusion | flops 98304 | bytes 131328 | tf_op jit(solution)/shard_map/convert_element_type | solution.py:47
  13.6 0.0 all-gather.2.cloned.1.call-update
  13.6 0.0 all-reduce.6.cloned.1.call-start
  14.3 0.8 compare_select_fusion
  15.1 22.6 %all-reduce.4.cloned.1.call-done = f32[128,512]{1,0:T(8,128)} async-done(((f32[128,512]{1,0:T(8,128)}), f32[128,512]{1,0:T(8,128)}) %all-reduce.4.cloned.1.call-update) | async-done | bytes 262160 | tf_op jit(solution)/shard_map/psum | solution.py:43
  37.7 1.1 multiply_reduce_fusion.1
  38.8 16.0 %all-gather.2.cloned.1.call-done = bf16[1024,512]{1,0:T(8,128)(2,1)} async-done(((bf16[64,512]{1,0:T(8,128)(2,1)}), bf16[1024,512]{1,0:T(8,128)(2,1)}) %all-gather.2.cloned.1.call-update) | async-done | bytes 1048592 | tf_op jit(solution)/shard_map/all_gather | solution.py:61
  54.8 0.0 copy-start.3
  54.8 1.9 %fusion.11 = (f32[128]{0:T(128)S(1)}, f32[128,1024]{1,0:T(8,128)S(1)}) fusion(bf16[1024,512]{1,0:T(8,128)(2,1)} %all-gather.2.cloned.1.call-done, f32[128,512]{1,0:T(8,128)} %all-reduce.4.cloned.1.call-done, f32[128]{0:T(128)S(1)} %add_rsqrt_fusion.1, f32[]{:T(128)} %bitcast.7), kind=kOutput, calls=%fused_computation.40 | convolution fusion | flops 134610816 | bytes 1836036 | tf_op jit(solution)/shard_map/dot_general | solution.py:16
  56.8 0.0 copy-start.1
  56.8 5.1 %pmax.7 = f32[128]{0:T(128)S(1)} all-reduce(f32[128]{0:T(128)S(1)} %broadcast_maximum_fusion), channel_id=1, replica_groups=mesh['dp'=16,'tensor'=2] {'tensor'}, use_global_device_ids=true, to_apply=%region_4.5 | all-reduce | flops 128 | bytes 1024 | tf_op jit(solution)/shard_map/pmax | solution.py:63
  61.9 0.3 select_reduce_fusion
  62.2 4.9 %all-reduce = (f32[128]{0:T(128)S(1)}, f32[128]{0:T(128)S(1)}) all-reduce(f32[128]{0:T(128)S(1)} %exponential_multiply_fusion, f32[128]{0:T(128)S(1)} %get-tuple-element.3), channel_id=1, replica_groups=mesh['dp'=16,'tensor'=2] {'tensor'}, use_global_device_ids=true, to_apply=%region_6.7 | all-reduce | flops 256 | bytes 2048 | tf_op jit(solution)/shard_map/psum | solution.py:64
  67.1 0.0 copy-done.3
  67.1 1.1 convolution_multiply_fusion.2
  68.2 0.0 all-reduce.6.cloned.1.call-update
  68.2 0.0 reduce-scatter.2.cloned.1.call-start
  68.3 0.0 copy-done.1
  68.3 2.0 %convolution_multiply_fusion = f32[1024,512]{1,0:T(8,128)} fusion(f32[]{:T(128)} %bitcast.8, f32[128,512]{1,0:T(8,128)S(1)} %copy-done.1, f32[128]{0:T(128)S(1)} %add_rsqrt_fusion.1, f32[128,1024]{1,0:T(8,128)S(1)} %get-tuple-element.8, s32[128]{0:T(128)S(1)} %compare_select_fusion, f32[128]{0:T(128)S(1)} %get-tuple-element.5, f32[128]{0:T(128)S(1)} %pmax.7), kind=kOutput, calls=%fused_computation | convolution fusion | flops 135659520 | bytes 2885636 | tf_op jit(solution)/shard_map/dot_general | solution.py:68
  70.2 0.0 copy-start.2
  70.2 0.0 reduce-scatter.2.cloned.1.call-update
  70.3 0.5 add_subtract_fusion
  70.8 19.9 %all-reduce.6.cloned.1.call-done = f32[128,512]{1,0:T(8,128)} async-done(((f32[128,512]{1,0:T(8,128)}), f32[128,512]{1,0:T(8,128)}) %all-reduce.6.cloned.1.call-update) | async-done | bytes 262160 | tf_op jit(solution)/shard_map/psum | solution.py:67
  90.7 1.1 multiply_reduce_fusion
  91.8 2.0 %fusion.7 = f32[128,640]{1,0:T(8,128)} fusion(bf16[640,512]{1,0:T(8,128)(2,1)S(1)} %copy-done, f32[128,512]{1,0:T(8,128)} %all-reduce.6.cloned.1.call-done, f32[128,512]{1,0:T(8,128)S(1)} %copy-done.1, f32[128]{0:T(128)S(1)} %multiply_reduce_fusion, f32[128]{0:T(128)S(1)} %add_rsqrt_fusion.1), kind=kOutput, calls=%fused_computation.20 | convolution fusion | flops 84213760 | bytes 1508352 | tf_op jit(solution)/shard_map/dot_general | solution.py:74
  93.9 39.4 %reduce-scatter.2.cloned.1.call-done = f32[64,512]{1,0:T(8,128)} async-done(((f32[1024,512]{1,0:T(8,128)}), f32[64,512]{1,0:T(8,128)}) %reduce-scatter.2.cloned.1.call-update) | async-done | bytes 131088 | tf_op jit(solution)/shard_map/reduce_scatter | solution.py:71
  133.3 0.0 copy-done.2
  133.3 1.1 fusion.3
  134.3 1.7 %fusion.5 = f32[64,512]{1,0:T(8,128)} fusion(f32[64,512]{1,0:T(8,128)} %reduce-scatter.2.cloned.1.call-done, bf16[64,512]{1,0:T(8,128)(2,1)S(1)} %copy-done.2, f32[64]{0:T(128)S(1)} %fusion.3, f32[64]{0:T(128)S(1)} %add_rsqrt_fusion), kind=kLoop, calls=%fused_computation.18 | loop fusion | flops 163840 | bytes 328192 | tf_op jit(solution)/shard_map/mul | solution.py:78
  (4 shorter events, 0.0 us)
Async XLA Ops:
  8.0 1.1 copy-start
  8.0 29.7 %all-reduce.4.cloned.1.call-start = ((), (), s32[]{:S(2)}) async-start(), calls=%async_computation.1 | async-start | bytes 524288 | tf_op jit(solution)/shard_map/psum | solution.py:43
  11.0 43.8 %all-gather.2.cloned.1.call-start = ((), (), s32[]{:S(2)}) async-start(), calls=%async_computation.2 | async-start | bytes 1114112 | tf_op jit(solution)/shard_map/all_gather | solution.py:61
  13.6 77.1 %all-reduce.6.cloned.1.call-start = ((), (), s32[]{:S(2)}) async-start(), calls=%async_computation.3 | async-start | bytes 524288 | tf_op jit(solution)/shard_map/psum | solution.py:67
  54.8 12.3 %copy-start.3 = (bf16[1024,512]{1,0:T(8,128)(2,1)S(1)}, bf16[1024,512]{1,0:T(8,128)(2,1)}, u32[]{:S(2)}) copy-start(bf16[1024,512]{1,0:T(8,128)(2,1)} %all-gather.2.cloned.1.call-done) | copy-start | bytes 3145732
  56.8 11.5 %copy-start.1 = (f32[128,512]{1,0:T(8,128)S(1)}, f32[128,512]{1,0:T(8,128)}, u32[]{:S(2)}) copy-start(f32[128,512]{1,0:T(8,128)} %all-reduce.4.cloned.1.call-done) | copy-start | bytes 786436
  68.2 65.0 %reduce-scatter.2.cloned.1.call-start = ((), (), s32[]{:S(2)}) async-start(), calls=%async_computation.4 | async-start | bytes 2228224 | tf_op jit(solution)/shard_map/reduce_scatter | solution.py:71
  70.2 63.0 %copy-start.2 = (bf16[64,512]{1,0:T(8,128)(2,1)S(1)}, bf16[64,512]{1,0:T(8,128)(2,1)}, u32[]{:S(2)}) copy-start(bf16[64,512]{1,0:T(8,128)(2,1)} %param.7) | copy-start | bytes 196612
Sparse Core Ops, SparseCore 0:
  11.7 26.0 all-reduce.3
  68.3 22.3 all-reduce.5
Sparse Core Ops, SparseCore 1:
  14.2 40.6 all-gather.1
  72.4 60.8 reduce-scatter.1
where the time goes:
time: 144 us; the launch traced here: 143 us
  waiting for transfers between devices  98 us (68%)
  between operations  16.2 us (11%)
  blocking collectives  10 us (7%)
  other arithmetic  9.03 us (6%)
  matrix products  8.93 us (6%)
    reduce_scatter x1, waiting for transfers between devices, body(): cap_grad = lax.psum_scatter(cap_part, 'dp', scatter_dimension=0, tiled=True)  39.4 us
    psum x1, waiting for transfers between devices, body(): raw_proj = lax.psum(partial_value, 'tensor')  22.6 us
    psum x1, waiting for transfers between devices, body(): vid_grad = lax.psum(vid_part, 'tensor')  19.9 us
    all_gather x1, waiting for transfers between devices, body(): gathered = lax.all_gather(captions, 'dp', axis=0, tiled=True)  16 us
    pmax x1, blocking collectives, body(): row_max = lax.pmax(stats[0], 'tensor')  5.07 us
    psum x1, blocking collectives, body(): lax.psum((stats[1] * jnp.exp(stats[0] - row_max), stats[2]), 'tensor')  4.93 us
  transfers between devices with their start and end apart: 4, of which 4 were waited for; matrix products, arithmetic and copies ran while one was open for 7% of the time, Pallas kernels for 0%

commit v1 on v0

--- a/solution.py
+++ b/solution.py
@@ -2,6 +2,7 @@
 import jax.numpy as jnp
 from jax import lax
 from jax.sharding import PartitionSpec as P
+from jax.lax import ppermute
 
 norm_eps = 1e-06
 
@@ -40,7 +41,11 @@
 def body(clip_feats, proj_weight, caption_emb, logit_scale, pair_perm):
     logit = logit_scale[0]
     partial_value = jnp.dot(clip_feats, proj_weight, preferred_element_type=jnp.float32)
-    raw_proj = lax.psum(partial_value, "tensor")
+
+    def shards_group(message):
+        return message + ppermute(message, "tensor", [(0, 1), (1, 0)])
+
+    raw_proj = shards_group(partial_value)
     unit_vid, vid_inv = unit_rows(raw_proj)
     videos = unit_vid.astype(jnp.bfloat16)
     cap_unit, cap_inv = unit_rows(caption_emb.astype(jnp.float32))

time: 144 us -> 162 us (1.12)
  waiting for transfers between devices: 98 us -> 118 us
  starting transfers between devices: 0.17 us -> 3.15 us
  between operations: 16.2 us -> 14.5 us
    reduce_scatter x1, waiting for transfers between devices: 39.4 us -> 62.4 us  [body(): cap_grad = lax.psum_scatter(cap_part, 'dp', scatter_dimension=0, tiled=True)]
    psum x1 -> x0, waiting for transfers between devices: 22.6 us -> none  [body(): raw_proj = lax.psum(partial_value, 'tensor')]
    all_gather x1, waiting for transfers between devices: 16 us -> 30.8 us  [body(): gathered = lax.all_gather(captions, 'dp', axis=0, tiled=True)]
    ppermute x0 -> x1, waiting for transfers between devices: none -> 4.87 us  [shards_group(): return message + ppermute(message, 'tensor', [(0, 1), (1, 0)])]
    ppermute x0 -> x1, starting transfers between devices: none -> 3.03 us  [shards_group(): return message + ppermute(message, 'tensor', [(0, 1), (1, 0)])]
  transfers between devices with their start and end apart: 4 -> 4, of which waited for: 4 -> 4; matrix products, arithmetic and copies ran while one was open for 7% -> 5% of each run, Pallas kernels for 0% -> 0%
where the time goes in v1:
time: 162 us
  waiting for transfers between devices  118 us (73%)
  between operations  14.5 us (9%)
  blocking collectives  9.87 us (6%)
  matrix products  8.16 us (5%)
  other arithmetic  8.14 us (5%)
  starting transfers between devices  3.15 us (2%)
    reduce_scatter x1, waiting for transfers between devices, body(): cap_grad = lax.psum_scatter(cap_part, 'dp', scatter_dimension=0, tiled=True)  62.4 us
    all_gather x1, waiting for transfers between devices, body(): gathered = lax.all_gather(captions, 'dp', axis=0, tiled=True)  30.8 us
    psum x1, waiting for transfers between devices, body(): vid_grad = lax.psum(vid_part, 'tensor')  19.9 us
    pmax x1, blocking collectives, body(): row_max = lax.pmax(stats[0], 'tensor')  4.93 us
    psum x1, blocking collectives, body(): lax.psum((stats[1] * jnp.exp(stats[0] - row_max), stats[2]), 'tensor')  4.93 us
    ppermute x1, waiting for transfers between devices, shards_group(): return message + ppermute(message, 'tensor', [(0, 1), (1, 0)])  4.87 us
  transfers between devices with their start and end apart: 4, of which 4 were waited for; matrix products, arithmetic and copies ran while one was open for 5% of the time, Pallas kernels for 0%

profile of v1, /device:TPU:0, one launch (start us, length us, event | category | flops | bytes accessed | tf_op | source)
XLA Modules:
  0.0 161.8 jit_solution(6086353623730253822)
XLA Ops:
  7.2 0.0 copy-start
  7.2 0.0 all-gather.2.cloned.1.call-start
  7.2 1.0 fusion.6
  8.3 1.6 fusion.2
  9.8 0.0 all-gather.2.cloned.1.call-update
  9.8 0.0 all-reduce.3.cloned.1.call-start
  9.9 0.0 copy-done
  9.9 1.2 fusion.12
  11.1 3.0 %collective-permute-start = (f32[128,512]{1,0:T(8,128)S(1)}, f32[128,512]{1,0:T(8,128)S(1)}, u32[]{:S(2)}, u32[]{:S(2)}) collective-permute-start(f32[128,512]{1,0:T(8,128)S(1)} %fusion.12), channel_id=1, source_target_pairs={{0,1},{1,0},{2,3},{3,2},{4,5},{5,4},{6,7},{7,6},{8,9},{9,8},{10,11... | collective-permute-start | bytes 786440 | tf_op jit(solution)/shard_map/ppermute | solution.py:46
  14.8 0.8 compare_select_fusion
  15.5 4.9 %collective-permute-done = f32[128,512]{1,0:T(8,128)S(1)} collective-permute-done((f32[128,512]{1,0:T(8,128)S(1)}, f32[128,512]{1,0:T(8,128)S(1)}, u32[]{:S(2)}, u32[]{:S(2)}) %collective-permute-start) | collective-permute-done | bytes 262176 | tf_op jit(solution)/shard_map/ppermute | solution.py:46
  20.4 0.1 multiply_reduce_fusion.1
  20.5 30.8 %all-gather.2.cloned.1.call-done = bf16[1024,512]{1,0:T(8,128)(2,1)} async-done(((bf16[64,512]{1,0:T(8,128)(2,1)}), bf16[1024,512]{1,0:T(8,128)(2,1)}) %all-gather.2.cloned.1.call-update) | async-done | bytes 1048592 | tf_op jit(solution)/shard_map/all_gather | solution.py:66
  51.3 0.0 copy-start.2
  51.3 1.9 %fusion.11 = (f32[128]{0:T(128)S(1)}, f32[128,1024]{1,0:T(8,128)S(1)}) fusion(bf16[1024,512]{1,0:T(8,128)(2,1)} %all-gather.2.cloned.1.call-done, f32[128,512]{1,0:T(8,128)S(1)} %get-tuple-element.8, f32[128]{0:T(128)S(1)} %add_rsqrt_fusion.1, f32[]{:T(128)} %bitcast.7), kind=kOutput, calls=%fused_computation.40 | convolution fusion | flops 134610816 | bytes 1836036 | tf_op jit(solution)/shard_map/dot_general | solution.py:17
  53.2 4.9 %pmax.7 = f32[128]{0:T(128)S(1)} all-reduce(f32[128]{0:T(128)S(1)} %broadcast_maximum_fusion), channel_id=1, replica_groups=mesh['dp'=16,'tensor'=2] {'tensor'}, use_global_device_ids=true, to_apply=%region_3.4 | all-reduce | flops 128 | bytes 1024 | tf_op jit(solution)/shard_map/pmax | solution.py:68
  58.1 0.3 select_reduce_fusion
  58.4 4.9 %all-reduce = (f32[128]{0:T(128)S(1)}, f32[128]{0:T(128)S(1)}) all-reduce(f32[128]{0:T(128)S(1)} %exponential_multiply_fusion, f32[128]{0:T(128)S(1)} %get-tuple-element.3), channel_id=1, replica_groups=mesh['dp'=16,'tensor'=2] {'tensor'}, use_global_device_ids=true, to_apply=%region_5.6 | all-reduce | flops 256 | bytes 2048 | tf_op jit(solution)/shard_map/psum | solution.py:69
  63.4 0.0 copy-done.2
  63.4 1.1 convolution_multiply_fusion.2
  64.5 0.0 all-reduce.3.cloned.1.call-update
  64.5 0.0 reduce-scatter.2.cloned.1.call-start
  64.5 2.0 %convolution_multiply_fusion = f32[1024,512]{1,0:T(8,128)} fusion(f32[]{:T(128)} %bitcast.8, f32[128,512]{1,0:T(8,128)S(1)} %get-tuple-element.8, f32[128]{0:T(128)S(1)} %add_rsqrt_fusion.1, f32[128,1024]{1,0:T(8,128)S(1)} %get-tuple-element.10, s32[128]{0:T(128)S(1)} %compare_select_fusion, f32[128]{0:T(128)S(1)} %get-tuple-element.5, f32[128]{0:T(128)S(1)} %pmax.7), kind=kOutput, calls=%fused_computation | convolution fusion | flops 135659520 | bytes 2885636 | tf_op jit(solution)/shard_map/dot_general | solution.py:73
  66.5 0.0 copy-start.1
  66.5 0.0 reduce-scatter.2.cloned.1.call-update
  66.5 0.5 add_subtract_fusion
  67.0 19.9 %all-reduce.3.cloned.1.call-done = f32[128,512]{1,0:T(8,128)} async-done(((f32[128,512]{1,0:T(8,128)}), f32[128,512]{1,0:T(8,128)}) %all-reduce.3.cloned.1.call-update) | async-done | bytes 262160 | tf_op jit(solution)/shard_map/psum | solution.py:72
  86.9 1.1 multiply_reduce_fusion
  88.0 2.0 %fusion.7 = f32[128,640]{1,0:T(8,128)} fusion(bf16[640,512]{1,0:T(8,128)(2,1)S(1)} %copy-done, f32[128,512]{1,0:T(8,128)} %all-reduce.3.cloned.1.call-done, f32[128,512]{1,0:T(8,128)S(1)} %get-tuple-element.8, f32[128]{0:T(128)S(1)} %multiply_reduce_fusion, f32[128]{0:T(128)S(1)} %add_rsqrt_fusion.1), kind=kOutput, calls=%fused_computation.20 | convolution fusion | flops 84213760 | bytes 1508352 | tf_op jit(solution)/shard_map/dot_general | solution.py:79
  90.1 62.4 %reduce-scatter.2.cloned.1.call-done = f32[64,512]{1,0:T(8,128)} async-done(((f32[1024,512]{1,0:T(8,128)}), f32[64,512]{1,0:T(8,128)}) %reduce-scatter.2.cloned.1.call-update) | async-done | bytes 131088 | tf_op jit(solution)/shard_map/reduce_scatter | solution.py:76
  152.5 0.0 copy-done.1
  152.5 1.1 fusion.3
  153.6 1.7 %fusion.5 = f32[64,512]{1,0:T(8,128)} fusion(f32[64,512]{1,0:T(8,128)} %reduce-scatter.2.cloned.1.call-done, bf16[64,512]{1,0:T(8,128)(2,1)S(1)} %copy-done.1, f32[64]{0:T(128)S(1)} %fusion.3, f32[64]{0:T(128)S(1)} %add_rsqrt_fusion), kind=kLoop, calls=%fused_computation.18 | loop fusion | flops 163840 | bytes 328192 | tf_op jit(solution)/shard_map/mul | solution.py:83
  (4 shorter events, 0.0 us)
Async XLA Ops:
  7.2 2.7 %copy-start = (bf16[640,512]{1,0:T(8,128)(2,1)S(1)}, bf16[640,512]{1,0:T(8,128)(2,1)}, u32[]{:S(2)}) copy-start(bf16[640,512]{1,0:T(8,128)(2,1)} %param.6) | copy-start | bytes 1966084
  7.2 44.1 %all-gather.2.cloned.1.call-start = ((), (), s32[]{:S(2)}) async-start(), calls=%async_computation.1 | async-start | bytes 1114112 | tf_op jit(solution)/shard_map/all_gather | solution.py:66
  9.8 77.1 %all-reduce.3.cloned.1.call-start = ((), (), s32[]{:S(2)}) async-start(), calls=%async_computation.2 | async-start | bytes 524288 | tf_op jit(solution)/shard_map/psum | solution.py:72
  11.1 9.3 %collective-permute-start = (f32[128,512]{1,0:T(8,128)S(1)}, f32[128,512]{1,0:T(8,128)S(1)}, u32[]{:S(2)}, u32[]{:S(2)}) collective-permute-start(f32[128,512]{1,0:T(8,128)S(1)} %fusion.12), channel_id=1, source_target_pairs={{0,1},{1,0},{2,3},{3,2},{4,5},{5,4},{6,7},{7,6},{8,9},{9,8},{10,11... | collective-permute-start | bytes 786440 | tf_op jit(solution)/shard_map/ppermute | solution.py:46
  51.3 12.0 %copy-start.2 = (bf16[1024,512]{1,0:T(8,128)(2,1)S(1)}, bf16[1024,512]{1,0:T(8,128)(2,1)}, u32[]{:S(2)}) copy-start(bf16[1024,512]{1,0:T(8,128)(2,1)} %all-gather.2.cloned.1.call-done) | copy-start | bytes 3145732
  64.5 88.0 %reduce-scatter.2.cloned.1.call-start = ((), (), s32[]{:S(2)}) async-start(), calls=%async_computation.3 | async-start | bytes 2228224 | tf_op jit(solution)/shard_map/reduce_scatter | solution.py:76
  66.5 86.0 %copy-start.1 = (bf16[64,512]{1,0:T(8,128)(2,1)S(1)}, bf16[64,512]{1,0:T(8,128)(2,1)}, u32[]{:S(2)}) copy-start(bf16[64,512]{1,0:T(8,128)(2,1)} %param.7) | copy-start | bytes 196612
Sparse Core Ops, SparseCore 0:
  10.7 40.5 all-gather.1
  64.6 22.2 all-reduce.2
  90.7 61.8 reduce-scatter.1
